TPU v7x, 32 devices: a whole 2x2x4 slice. The times are simulated.
32 devices in a mesh: hid: 4 (over y, x), tok: 8 (over z, core).
Axes of the slice: x: 2, y: 2, z: 4, core: 2. Of those that a mesh axis runs over, the one named last changes fastest.
Arguments:
- keys: bfloat16 [2, 512, 1280], P(None, 'tok'), may hold values from -6 to 6
- values: bfloat16 [2, 512, 1280], P(None, 'tok'), may hold values from -6 to 6
- queries: bfloat16 [512, 1280], P('tok'), may hold values from -6 to 6
- rates: float32 [2, 512], P(None, 'tok'), may hold values from 0.01 to 0.1
- forget: float32 [2], replicated, may hold values from 0.05 to 0.3
- momentum: float32 [1], replicated, may hold values from 0.5 to 0.95
- write_weight: float32 [1280, 1280], P('tok', 'hid'), may hold values from -0.15625 to 0.15625
- read_weight: float32 [1280, 1280], P('tok', 'hid'), may hold values from -0.15625 to 0.15625
Outputs:
- new_write: float32 [1280, 1280], P('tok', 'hid')
- new_read: float32 [1280, 1280], P('tok', 'hid')
- recalled: bfloat16 [512, 1280], P('tok')
All inputs are finite; a program needn't handle non-finite values.
Results may differ from a plain program's by a relative error of at most 0.003.
Values may be sent and summed in bfloat16 or wider, within the bound.
No kernel may reach another device: no remote copies, remote signals or barrier semaphores. Data moves between devices by JAX's collectives and lax.ppermute only.
A program may use at most 64 MiB of HBM per device.

v0:
```python
import jax
import jax.numpy as jnp
from jax import lax
from jax.sharding import PartitionSpec as P

highest = lax.Precision.HIGHEST
radius = 12.0


def silu_slope(z):
    sig = jax.nn.sigmoid(z)
    return sig * (1.0 + z * (1.0 - sig))


def times_transposed(left, right):
    return lax.dot_general(left, right, (((1,), (1,)), ((), ())), precision=highest)


def inner_rows(left, right):
    return lax.dot_general(left, right, (((0,), (0,)), ((), ())), precision=highest)


def on_device(keys, values, queries, rates, forget, momentum, write_weight, read_weight):
    width = keys.shape[2]
    full_write, full_read = (
        lax.all_gather(write_weight, "tok", axis=0, tiled=True),
        lax.all_gather(read_weight, "tok", axis=0, tiled=True),
    )
    inputs = keys.reshape(-1, width).astype(jnp.float32)
    hidden_pre = jnp.dot(inputs, full_write, precision=highest)
    hidden = jax.nn.silu(hidden_pre)
    output = lax.psum(times_transposed(hidden, full_read).astype(jnp.bfloat16), "hid").astype(
        jnp.float32
    )
    error = inputs + output - values.reshape(-1, width).astype(jnp.float32)
    factor = 1.0 - forget[1] + momentum[0]
    per_block = jnp.stack([factor, jnp.ones_like(factor)])
    row_scale = (2.0 * rates * per_block[:, None]).reshape(-1, 1)
    delta = row_scale * error
    back = jnp.dot(delta, full_read, precision=highest) * silu_slope(hidden_pre)
    grad_write = inner_rows(inputs, back)
    grad_read = inner_rows(delta, hidden)
    part_w, part_r = (
        lax.psum_scatter(grad_write, "tok", scatter_dimension=0, tiled=True),
        lax.psum_scatter(grad_read, "tok", scatter_dimension=0, tiled=True),
    )
    keep = (1.0 - forget[0]) * (1.0 - forget[1])
    whole_w, whole_r = (
        lax.all_gather(part_w, "tok", axis=0, tiled=True),
        lax.all_gather(part_r, "tok", axis=0, tiled=True),
    )
    total = lax.psum(jnp.sum(whole_w * whole_w) + jnp.sum(whole_r * whole_r), "hid")
    scale = jnp.minimum(1.0, radius / jnp.sqrt(total + 1e-06))
    new_write = keep * write_weight - scale * part_w
    new_read = keep * read_weight - scale * part_r
    wide_write = keep * full_write - scale * whole_w
    wide_read = keep * full_read - scale * whole_r
    asked = queries.astype(jnp.float32)
    query_hidden = jax.nn.silu(jnp.dot(asked, wide_write, precision=highest))
    answer = lax.psum(times_transposed(query_hidden, wide_read), "hid")
    recalled = (asked + answer).astype(jnp.bfloat16)
    return (new_write, new_read, recalled)


def solution(mesh):
    in_specs = (
        P(None, "tok", None),
        P(None, "tok", None),
        P("tok", None),
        P(None, "tok"),
        P(),
        P(),
        P("tok", "hid"),
        P("tok", "hid"),
    )
    out_specs = (P("tok", "hid"), P("tok", "hid"), P("tok", None))
    return jax.shard_map(
        on_device, mesh=mesh, in_specs=in_specs, out_specs=out_specs, check_vma=False
    )
```

profile of v0, /device:TPU:0, one launch (start us, length us, event | category | flops | bytes accessed | tf_op | source)
XLA Modules:
  0.0 327.0 jit_solution(6038212173051882562)
XLA Ops:
  7.9 0.7 all-gather.7.cloned.1.call-update
  9.3 1.3 fusion.33
  11.3 29.1 %all-gather.5.cloned.1.call-done = f32[1280,320]{1,0:T(8,128)} async-done(((f32[160,320]{1,0:T(8,128)}), f32[1280,320]{1,0:T(8,128)}) %all-gather.5.cloned.1.call-update) | async-done | bytes 1638416 | tf_op jit(solution)/shard_map/all_gather | solution.py:26
  40.4 3.4 %fusion.34 = f32[128,320]{0,1:T(8,128)S(1)} fusion(bf16[128,1280]{1,0:T(8,128)(2,1)} %bitcast.17, f32[1280,320]{1,0:T(8,128)} %all-gather.5.cloned.1.call-done), kind=kOutput, calls=%fused_computation.40 | convolution fusion | flops 629145600 | bytes 2129920 | tf_op jit(solution)/shard_map/dot_general | solution.py:30
  43.8 25.7 %all-gather.7.cloned.1.call-done = f32[1280,320]{1,0:T(8,128)} async-done(((f32[160,320]{1,0:T(8,128)}), f32[1280,320]{1,0:T(8,128)}) %all-gather.7.cloned.1.call-update) | async-done | bytes 1638416 | tf_op jit(solution)/shard_map/all_gather | solution.py:27
  69.6 4.6 %convolution_convert_fusion = bf16[128,1280]{1,0:T(8,128)(2,1)} fusion(f32[1280,320]{1,0:T(8,128)} %all-gather.7.cloned.1.call-done, f32[128,320]{0,1:T(8,128)S(1)} %fusion.34), kind=kOutput, calls=%fused_computation.1 | convolution fusion | flops 629473280 | bytes 2129920 | tf_op jit(solution)/shard_map/dot_general | solution.py:16
  74.5 42.8 %all-reduce.3.cloned.1.call-done = bf16[128,1280]{1,0:T(8,128)(2,1)} async-done(((bf16[128,1280]{1,0:T(8,128)(2,1)}), bf16[128,1280]{1,0:T(8,128)(2,1)}) %all-reduce.3.cloned.1.call-update) | async-done | bytes 327696 | tf_op jit(solution)/shard_map/psum | solution.py:32
  117.4 4.3 %convolution_multiply_fusion = f32[128,320]{0,1:T(8,128)S(1)} fusion(f32[1280,320]{1,0:T(8,128)S(1)} %copy-done, bf16[128,1280]{1,0:T(8,128)(2,1)S(1)} %bitcast.21, bf16[128,1280]{1,0:T(8,128)(2,1)} %all-reduce.3.cloned.1.call-done, bf16[128,1280]{1,0:T(8,128)(2,1)S(1)} %bitcast.18, f32[128]{0:T(128)S(1)} %mul.101, f32[128,320]{0,1:T(8,128)S(1)} %fusion.34), kind=kOutput, calls=%fused_computation.12 | convolution fusion | flops 630456320 | bytes 2949632 | tf_op jit(solution)/shard_map/dot_general | solution.py:40
  121.6 2.0 convolution_bitcast_fusion
  123.6 2.8 copy.26
  126.5 3.7 %fusion.16 = f32[1280,320]{1,0:T(8,128)} fusion(bf16[128,1280]{1,0:T(8,128)(2,1)S(1)} %bitcast.22, bf16[128,1280]{1,0:T(8,128)(2,1)S(1)} %copy-done.4, bf16[128,1280]{1,0:T(8,128)(2,1)S(1)} %bitcast.20, f32[128]{0:T(128)S(1)} %mul.101, f32[128,320]{0,1:T(8,128)S(1)} %fusion.34), kind=kOutput, calls=%fused_computation.20 | convolution fusion | flops 630292480 | bytes 2785792
  130.3 32.2 %reduce-scatter.7.cloned.1.call-done = f32[160,320]{1,0:T(8,128)} async-done(((f32[1280,320]{1,0:T(8,128)}), f32[160,320]{1,0:T(8,128)}) %reduce-scatter.7.cloned.1.call-update) | async-done | bytes 204816 | tf_op jit(solution)/shard_map/reduce_scatter | solution.py:44
  162.5 36.2 %reduce-scatter.9.cloned.1.call-done = f32[160,320]{1,0:T(8,128)} async-done(((f32[1280,320]{1,0:T(8,128)}), f32[160,320]{1,0:T(8,128)}) %reduce-scatter.9.cloned.1.call-update) | async-done | bytes 204816 | tf_op jit(solution)/shard_map/reduce_scatter | solution.py:45
  199.5 27.1 %all-gather.9.cloned.1.call-done = f32[1280,320]{1,0:T(8,128)} async-done(((f32[160,320]{1,0:T(8,128)}), f32[1280,320]{1,0:T(8,128)}) %all-gather.9.cloned.1.call-update) | async-done | bytes 1638416 | tf_op jit(solution)/shard_map/all_gather | solution.py:49
  226.6 2.7 multiply_reduce_fusion.1
  229.3 26.5 %all-gather.11.cloned.1.call-done = f32[1280,320]{1,0:T(8,128)} async-done(((f32[160,320]{1,0:T(8,128)}), f32[1280,320]{1,0:T(8,128)}) %all-gather.11.cloned.1.call-update) | async-done | bytes 1638416 | tf_op jit(solution)/shard_map/all_gather | solution.py:50
  255.7 2.7 multiply_reduce_fusion
  259.7 10.5 %psum.22 = f32[]{:T(128)} all-reduce(f32[]{:T(128)S(6)} %add.42), channel_id=1, replica_groups=mesh['hid'=4,'tok'=8] {'hid'}, use_global_device_ids=true, to_apply=%region_5.6 | all-reduce | flops 1 | bytes 8 | tf_op jit(solution)/shard_map/psum | solution.py:52
  270.9 3.3 %fusion.8 = f32[64,320]{1,0:T(8,128)S(1)} fusion(bf16[64,1280]{1,0:T(8,128)(2,1)S(1)} %copy-done.9, f32[1280,320]{1,0:T(8,128)} %all-gather.9.cloned.1.call-done, f32[1280,320]{1,0:T(8,128)} %all-gather.5.cloned.1.call-done, f32[]{:T(128)S(6)} %min.3, f32[]{:T(128)} %bitcast), kind=kOutput, calls=%fused_computation.13 | convolution fusion | flops 315801600 | bytes 3522568 | tf_op jit(solution)/shard_map/dot_general | solution.py:59
  274.3 2.9 fusion
  278.4 0.8 copy.23
  279.2 0.8 copy.24
  280.0 38.5 %all-reduce.5.cloned.1.call-done = f32[64,1280]{1,0:T(8,128)} async-done(((f32[64,1280]{1,0:T(8,128)}), f32[64,1280]{1,0:T(8,128)}) %all-reduce.5.cloned.1.call-update) | async-done | bytes 327696 | tf_op jit(solution)/shard_map/psum | solution.py:60
  318.5 1.7 add_convert_fusion
  (45 shorter events, 2.5 us)
Async XLA Ops:
  7.2 33.3 %all-gather.5.cloned.1.call-start = ((), (), s32[]{:S(2)}) async-start(), calls=%async_computation.2 | async-start | bytes 2211840 | tf_op jit(solution)/shard_map/all_gather | solution.py:26
  7.9 61.7 %all-gather.7.cloned.1.call-start = ((), (), s32[]{:S(2)}) async-start(), calls=%async_computation.3 | async-start | bytes 2211840 | tf_op jit(solution)/shard_map/all_gather | solution.py:27
  8.6 108.7 %all-reduce.3.cloned.1.call-start = ((), (), s32[]{:S(2)}) async-start(), calls=%async_computation.4 | async-start | bytes 655360 | tf_op jit(solution)/shard_map/psum | solution.py:32
  43.8 30.5 %copy-start.10 = (f32[2,64]{1,0:T(2,128)S(1)}, f32[2,64]{1,0:T(2,128)}, u32[]{:S(2)}) copy-start(f32[2,64]{1,0:T(2,128)} %param.11) | copy-start | bytes 1540
  43.8 73.5 %copy-start.2 = (bf16[2,64,1280]{2,1,0:T(8,128)(2,1)S(1)}, bf16[2,64,1280]{2,1,0:T(8,128)(2,1)}, u32[]{:S(2)}) copy-start(bf16[2,64,1280]{2,1,0:T(8,128)(2,1)} %param.8) | copy-start | bytes 983044
  43.8 73.5 %copy-start.3 = (bf16[2,64,1280]{2,1,0:T(8,128)(2,1)S(1)}, bf16[2,64,1280]{2,1,0:T(8,128)(2,1)}, u32[]{:S(2)}) copy-start(bf16[2,64,1280]{2,1,0:T(8,128)(2,1)} %param.9) | copy-start | bytes 983044
  69.6 47.8 %copy-start = (f32[1280,320]{1,0:T(8,128)S(1)}, f32[1280,320]{1,0:T(8,128)}, u32[]{:S(2)}) copy-start(f32[1280,320]{1,0:T(8,128)} %all-gather.7.cloned.1.call-done) | copy-start | bytes 4915204
  74.2 88.2 %reduce-scatter.7.cloned.1.call-start = ((), (), s32[]{:S(2)}) async-start(), calls=%async_computation.8 | async-start | bytes 2211840 | tf_op jit(solution)/shard_map/reduce_scatter | solution.py:44
  123.6 2.9 copy-start.4
  126.5 72.3 %reduce-scatter.9.cloned.1.call-start = ((), (), s32[]{:S(2)}) async-start(), calls=%async_computation.9 | async-start | bytes 2211840 | tf_op jit(solution)/shard_map/reduce_scatter | solution.py:45
  130.2 96.4 %all-gather.9.cloned.1.call-start = ((), (), s32[]{:S(2)}) async-start(), calls=%async_computation.5 | async-start | bytes 2211840 | tf_op jit(solution)/shard_map/all_gather | solution.py:49
  162.5 93.3 %all-gather.11.cloned.1.call-start = ((), (), s32[]{:S(2)}) async-start(), calls=%async_computation.6 | async-start | bytes 2211840 | tf_op jit(solution)/shard_map/all_gather | solution.py:50
  198.8 119.7 %all-reduce.5.cloned.1.call-start = ((), (), s32[]{:S(2)}) async-start(), calls=%async_computation.7 | async-start | bytes 655360 | tf_op jit(solution)/shard_map/psum | solution.py:60
  199.5 71.5 %copy-start.9 = (bf16[64,1280]{1,0:T(8,128)(2,1)S(1)}, bf16[64,1280]{1,0:T(8,128)(2,1)}, u32[]{:S(2)}) copy-start(bf16[64,1280]{1,0:T(8,128)(2,1)} %param.10) | copy-start | bytes 491524
  270.9 3.3 %copy-start.1 = (f32[1280,320]{1,0:T(8,128)S(1)}, f32[1280,320]{1,0:T(8,128)}, u32[]{:S(2)}) copy-start(f32[1280,320]{1,0:T(8,128)} %all-gather.11.cloned.1.call-done) | copy-start | bytes 4915204
  274.2 2.9 copy-start.5
  274.3 3.1 copy-start.6
  274.3 3.2 copy-start.7
  277.2 0.9 copy-start.8
Sparse Core Ops, SparseCore 0:
  9.6 30.7 all-gather.4
  42.1 27.4 all-gather.6
  74.3 42.9 all-reduce.2
  126.6 35.8 reduce-scatter.6
  164.6 34.0 reduce-scatter.8
  200.2 26.3 all-gather.8
  228.2 27.4 all-gather.10
  277.3 41.1 all-reduce.4
where the time goes:
time: 327 us
  waiting for transfers between devices  260 us (80%)
  matrix products  24 us (7%)
  between operations  18.3 us (6%)
  blocking collectives  10.5 us (3%)
  other arithmetic  7.21 us (2%)
  local copies, waits for them, and re-layouts  6.97 us (2%)
    psum x1, waiting for transfers between devices, on_device(): lax.psum(times_transposed(hidden, full_read).astype(jnp.bfloat16), 'hid')  42.8 us
    psum x1, waiting for transfers between devices, on_device(): answer = lax.psum(times_transposed(query_hidden, wide_read), 'hid')  38.5 us
    reduce_scatter x1, waiting for transfers between devices, on_device(): lax.psum_scatter(grad_read, 'tok', scatter_dimension=0, tiled=True)  36.2 us
    reduce_scatter x1, waiting for transfers between devices, on_device(): lax.psum_scatter(grad_write, 'tok', scatter_dimension=0, tiled=True)  32.2 us
    all_gather x1, waiting for transfers between devices, on_device(): lax.all_gather(write_weight, 'tok', axis=0, tiled=True)  29.1 us
    all_gather x1, waiting for transfers between devices, on_device(): lax.all_gather(part_w, 'tok', axis=0, tiled=True)  27.1 us
    all_gather x1, waiting for transfers between devices, on_device(): lax.all_gather(part_r, 'tok', axis=0, tiled=True)  26.5 us
    all_gather x1, waiting for transfers between devices, on_device(): lax.all_gather(read_weight, 'tok', axis=0, tiled=True)  25.7 us
  transfers between devices with their start and end apart: 8, of which 8 were waited for; matrix products, arithmetic and copies ran while one was open for 4% of the time, Pallas kernels for 0%

commit v1 on v0

--- a/solution.py
+++ b/solution.py
@@ -47,7 +47,9 @@
     keep = (1.0 - forget[0]) * (1.0 - forget[1])
     whole_w, whole_r = (
         lax.all_gather(part_w, "tok", axis=0, tiled=True),
-        lax.all_gather(part_r, "tok", axis=0, tiled=True),
+        jnp.concatenate(
+            lax.all_to_all(jnp.stack([part_r] * lax.axis_size("tok")), "tok", 0, 0), axis=0
+        ),
     )
     total = lax.psum(jnp.sum(whole_w * whole_w) + jnp.sum(whole_r * whole_r), "hid")
     scale = jnp.minimum(1.0, radius / jnp.sqrt(total + 1e-06))

time: 327 us -> 340 us (1.040)
  waiting for transfers between devices: 260 us -> 265 us
  starting transfers between devices: 0.32 us -> 4.6 us
  local copies, waits for them, and re-layouts: 6.97 us -> 10.7 us
    all_gather x1 -> x0, waiting for transfers between devices: 26.5 us -> none  [on_device(): lax.all_gather(part_r, 'tok', axis=0, tiled=True)]
    all_to_all x0 -> x1, waiting for transfers between devices: none -> 21.8 us  [on_device(): lax.all_to_all(jnp.stack([part_r] * lax.axis_size('tok')), 'tok', 0, 0)]
    all_gather x1, waiting for transfers between devices: 27.1 us -> 36.8 us  [on_device(): lax.all_gather(part_w, 'tok', axis=0, tiled=True)]
    all_to_all x0 -> x1, starting transfers between devices: none -> 4.32 us  [on_device(): lax.all_to_all(jnp.stack([part_r] * lax.axis_size('tok')), 'tok', 0, 0)]
    unnamed x29 -> x31, local copies, waits for them, and re-layouts: 5.57 us -> 7 us
  transfers between devices with their start and end apart: 8 -> 8, of which waited for: 8 -> 8; matrix products, arithmetic and copies ran while one was open for 4% -> 5% of each run, Pallas kernels for 0% -> 0%
where the time goes in v1:
time: 340 us
  waiting for transfers between devices  265 us (78%)
  matrix products  21.7 us (6%)
  between operations  18.3 us (5%)
  local copies, waits for them, and re-layouts  10.7 us (3%)
  blocking collectives  10.6 us (3%)
  other arithmetic  9.15 us (3%)
  starting transfers between devices  4.6 us (1%)
    psum x1, waiting for transfers between devices, on_device(): lax.psum(times_transposed(hidden, full_read).astype(jnp.bfloat16), 'hid')  42.8 us
    psum x1, waiting for transfers between devices, on_device(): answer = lax.psum(times_transposed(query_hidden, wide_read), 'hid')  38.3 us
    all_gather x1, waiting for transfers between devices, on_device(): lax.all_gather(part_w, 'tok', axis=0, tiled=True)  36.8 us
    reduce_scatter x1, waiting for transfers between devices, on_device(): lax.psum_scatter(grad_read, 'tok', scatter_dimension=0, tiled=True)  36.3 us
    reduce_scatter x1, waiting for transfers between devices, on_device(): lax.psum_scatter(grad_write, 'tok', scatter_dimension=0, tiled=True)  32.2 us
    all_gather x1, waiting for transfers between devices, on_device(): lax.all_gather(write_weight, 'tok', axis=0, tiled=True)  29.1 us
    all_gather x1, waiting for transfers between devices, on_device(): lax.all_gather(read_weight, 'tok', axis=0, tiled=True)  25.7 us
    all_to_all x1, waiting for transfers between devices, on_device(): lax.all_to_all(jnp.stack([part_r] * lax.axis_size('tok')), 'tok', 0, 0)  21.8 us
  transfers between devices with their start and end apart: 8, of which 8 were waited for; matrix products, arithmetic and copies ran while one was open for 5% of the time, Pallas kernels for 0%

profile of v1, /device:TPU:0, one launch (start us, length us, event | category | flops | bytes accessed | tf_op | source)
XLA Modules:
  0.0 339.7 jit_solution(4556793764941514454)
XLA Ops:
  9.3 1.3 fusion.28
  11.3 29.1 %all-gather.4.cloned.1.call-done = f32[1280,320]{1,0:T(8,128)} async-done(((f32[160,320]{1,0:T(8,128)}), f32[1280,320]{1,0:T(8,128)}) %all-gather.4.cloned.1.call-update) | async-done | bytes 1638416 | tf_op jit(solution)/shard_map/all_gather | solution.py:26
  40.4 3.4 fusion.29
  43.8 25.7 %all-gather.6.cloned.1.call-done = f32[1280,320]{1,0:T(8,128)} async-done(((f32[160,320]{1,0:T(8,128)}), f32[1280,320]{1,0:T(8,128)}) %all-gather.6.cloned.1.call-update) | async-done | bytes 1638416 | tf_op jit(solution)/shard_map/all_gather | solution.py:27
  69.6 4.6 %convolution_convert_fusion = bf16[128,1280]{1,0:T(8,128)(2,1)} fusion(f32[1280,320]{1,0:T(8,128)} %all-gather.6.cloned.1.call-done, f32[128,320]{0,1:T(8,128)S(1)} %fusion.29), kind=kOutput, calls=%fused_computation.1 | convolution fusion | flops 629473280 | bytes 2129920 | tf_op jit(solution)/shard_map/dot_general | solution.py:16
  74.5 42.8 %all-reduce.3.cloned.1.call-done = bf16[128,1280]{1,0:T(8,128)(2,1)} async-done(((bf16[128,1280]{1,0:T(8,128)(2,1)}), bf16[128,1280]{1,0:T(8,128)(2,1)}) %all-reduce.3.cloned.1.call-update) | async-done | bytes 327696 | tf_op jit(solution)/shard_map/psum | solution.py:32
  117.4 4.3 %convolution_multiply_fusion = f32[128,320]{0,1:T(8,128)S(1)} fusion(f32[1280,320]{1,0:T(8,128)S(1)} %copy-done, bf16[128,1280]{1,0:T(8,128)(2,1)S(1)} %bitcast.24, bf16[128,1280]{1,0:T(8,128)(2,1)} %all-reduce.3.cloned.1.call-done, bf16[128,1280]{1,0:T(8,128)(2,1)S(1)} %bitcast.21, f32[128]{0:T(128)S(1)} %mul.107, f32[128,320]{0,1:T(8,128)S(1)} %fusion.29), kind=kOutput, calls=%fused_computation.9 | convolution fusion | flops 630456320 | bytes 2949632 | tf_op jit(solution)/shard_map/dot_general | solution.py:40
  121.6 2.0 convolution_bitcast_fusion
  123.6 2.8 copy.35
  126.5 3.7 %fusion.10 = f32[1280,320]{1,0:T(8,128)} fusion(bf16[128,1280]{1,0:T(8,128)(2,1)S(1)} %bitcast.25, bf16[128,1280]{1,0:T(8,128)(2,1)S(1)} %copy-done.5, bf16[128,1280]{1,0:T(8,128)(2,1)S(1)} %bitcast.23, f32[128]{0:T(128)S(1)} %mul.107, f32[128,320]{0,1:T(8,128)S(1)} %fusion.29), kind=kOutput, calls=%fused_computation.16 | convolution fusion | flops 630292480 | bytes 2785792
  130.3 32.2 %reduce-scatter.7.cloned.1.call-done = f32[160,320]{1,0:T(8,128)} async-done(((f32[1280,320]{1,0:T(8,128)}), f32[160,320]{1,0:T(8,128)}) %reduce-scatter.7.cloned.1.call-update) | async-done | bytes 204816 | tf_op jit(solution)/shard_map/reduce_scatter | solution.py:44
  162.5 36.3 %reduce-scatter.9.cloned.1.call-done = f32[160,320]{1,0:T(8,128)} async-done(((f32[1280,320]{1,0:T(8,128)}), f32[160,320]{1,0:T(8,128)}) %reduce-scatter.9.cloned.1.call-update) | async-done | bytes 204816 | tf_op jit(solution)/shard_map/reduce_scatter | solution.py:45
  198.8 2.3 stack.5
  201.1 4.3 %all-to-all-start = ((f32[8,160,320]{2,1,0:T(8,128)}), f32[8,160,320]{2,1,0:T(8,128)}, u32[]{:S(2)}, u32[]{:S(2)}) async-start(f32[8,160,320]{2,1,0:T(8,128)} %stack.5), calls=%async_computation | async-start | bytes 3932160 | tf_op jit(solution)/shard_map/all_to_all | solution.py:51
  206.1 36.8 %all-gather.8.cloned.1.call-done = f32[1280,320]{1,0:T(8,128)} async-done(((f32[160,320]{1,0:T(8,128)}), f32[1280,320]{1,0:T(8,128)}) %all-gather.8.cloned.1.call-update) | async-done | bytes 1638416 | tf_op jit(solution)/shard_map/all_gather | solution.py:49
  243.0 2.7 multiply_reduce_fusion.1
  245.6 21.8 %all-to-all-done = f32[8,160,320]{2,1,0:T(8,128)} async-done(((f32[8,160,320]{2,1,0:T(8,128)}), f32[8,160,320]{2,1,0:T(8,128)}, u32[]{:S(2)}, u32[]{:S(2)}) %all-to-all-start) | async-done | bytes 1638432 | tf_op jit(solution)/shard_map/all_to_all | solution.py:51
  267.5 2.7 multiply_reduce_fusion
  271.4 10.6 %psum.22 = f32[]{:T(128)} all-reduce(f32[]{:T(128)S(6)} %add.42), channel_id=1, replica_groups=mesh['hid'=4,'tok'=8] {'hid'}, use_global_device_ids=true, to_apply=%region_5.6 | all-reduce | flops 1 | bytes 8 | tf_op jit(solution)/shard_map/psum | solution.py:54
  282.7 1.7 broadcast_multiply_fusion
  284.6 1.3 copy-done.1
  287.6 2.8 fusion.16
  292.8 38.3 %all-reduce.5.cloned.1.call-done = f32[64,1280]{1,0:T(8,128)} async-done(((f32[64,1280]{1,0:T(8,128)}), f32[64,1280]{1,0:T(8,128)}) %all-reduce.5.cloned.1.call-update) | async-done | bytes 327696 | tf_op jit(solution)/shard_map/psum | solution.py:62
  331.1 1.7 add_convert_fusion
  (49 shorter events, 6.3 us)
Async XLA Ops:
  7.2 33.3 %all-gather.4.cloned.1.call-start = ((), (), s32[]{:S(2)}) async-start(), calls=%async_computation.3 | async-start | bytes 2211840 | tf_op jit(solution)/shard_map/all_gather | solution.py:26
  7.9 61.7 %all-gather.6.cloned.1.call-start = ((), (), s32[]{:S(2)}) async-start(), calls=%async_computation.4 | async-start | bytes 2211840 | tf_op jit(solution)/shard_map/all_gather | solution.py:27
  8.6 108.7 %all-reduce.3.cloned.1.call-start = ((), (), s32[]{:S(2)}) async-start(), calls=%async_computation.5 | async-start | bytes 655360 | tf_op jit(solution)/shard_map/psum | solution.py:32
  43.8 30.5 %copy-start.11 = (f32[2,64]{1,0:T(2,128)S(1)}, f32[2,64]{1,0:T(2,128)}, u32[]{:S(2)}) copy-start(f32[2,64]{1,0:T(2,128)} %param.11) | copy-start | bytes 1540
  43.8 73.5 %copy-start.3 = (bf16[2,64,1280]{2,1,0:T(8,128)(2,1)S(1)}, bf16[2,64,1280]{2,1,0:T(8,128)(2,1)}, u32[]{:S(2)}) copy-start(bf16[2,64,1280]{2,1,0:T(8,128)(2,1)} %param.8) | copy-start | bytes 983044
  43.8 73.5 %copy-start.4 = (bf16[2,64,1280]{2,1,0:T(8,128)(2,1)S(1)}, bf16[2,64,1280]{2,1,0:T(8,128)(2,1)}, u32[]{:S(2)}) copy-start(bf16[2,64,1280]{2,1,0:T(8,128)(2,1)} %param.9) | copy-start | bytes 983044
  69.6 47.8 %copy-start = (f32[1280,320]{1,0:T(8,128)S(1)}, f32[1280,320]{1,0:T(8,128)}, u32[]{:S(2)}) copy-start(f32[1280,320]{1,0:T(8,128)} %all-gather.6.cloned.1.call-done) | copy-start | bytes 4915204
  74.2 88.2 %reduce-scatter.7.cloned.1.call-start = ((), (), s32[]{:S(2)}) async-start(), calls=%async_computation.8 | async-start | bytes 2211840 | tf_op jit(solution)/shard_map/reduce_scatter | solution.py:44
  123.6 2.9 copy-start.5
  126.5 72.3 %reduce-scatter.9.cloned.1.call-start = ((), (), s32[]{:S(2)}) async-start(), calls=%async_computation.9 | async-start | bytes 2211840 | tf_op jit(solution)/shard_map/reduce_scatter | solution.py:45
  130.2 112.7 %all-gather.8.cloned.1.call-start = ((), (), s32[]{:S(2)}) async-start(), calls=%async_computation.6 | async-start | bytes 2211840 | tf_op jit(solution)/shard_map/all_gather | solution.py:49
  201.1 66.4 %all-to-all-start = ((f32[8,160,320]{2,1,0:T(8,128)}), f32[8,160,320]{2,1,0:T(8,128)}, u32[]{:S(2)}, u32[]{:S(2)}) async-start(f32[8,160,320]{2,1,0:T(8,128)} %stack.5), calls=%async_computation | async-start | bytes 3932160 | tf_op jit(solution)/shard_map/all_to_all | solution.py:51
  205.4 125.7 %all-reduce.5.cloned.1.call-start = ((), (), s32[]{:S(2)}) async-start(), calls=%async_computation.7 | async-start | bytes 655360 | tf_op jit(solution)/shard_map/psum | solution.py:62
  284.4 1.5 copy-start.1
  284.4 2.1 copy-start.2
  284.4 2.1 copy-start.10
  287.5 2.9 copy-start.6
  287.5 3.0 copy-start.7
  287.6 3.2 copy-start.8
  287.6 3.3 copy-start.9
Sparse Core Ops, SparseCore 0:
  9.6 30.7 all-gather.3
  42.1 27.4 all-gather.5
  74.3 42.9 all-reduce.2
  126.6 35.8 reduce-scatter.6
  164.6 34.0 reduce-scatter.8
  200.2 42.6 all-gather.7
  290.5 40.5 all-reduce.4
